TPU v7x, 32 devices: a whole 2x2x4 slice. The times are simulated.
32 devices in a mesh: dp: 8 (over z, x), tensor: 4 (over y, core).
Axes of the slice: x: 2, y: 2, z: 4, core: 2. Of those that a mesh axis runs over, the one named last changes fastest.
Arguments:
- inputs: bfloat16 [16, 1024, 1024], P('dp'), may hold values from -6 to 6
- segment_ids: int32 [16, 1024], P('dp'), may hold values from 0 to 7, never falling along the last dimension, each value on 1 to 512 neighbouring positions
- doc_offsets: int32 [16, 8], P('dp'), may hold values from 0 to 3071
- time_index: int32 [16], P('dp'), may hold values from 0 to 999
- w_qkv: bfloat16 [3, 1024, 1024], P(None, 'dp', 'tensor'), may hold values from -0.1875 to 0.1875
- w_out: bfloat16 [1024, 1024], P('tensor', 'dp'), may hold values from -0.75 to 0.75
- w_up: bfloat16 [1024, 4096], P('dp', 'tensor'), may hold values from -0.1875 to 0.1875
- w_down: bfloat16 [4096, 1024], P('tensor', 'dp'), may hold values from -0.09375 to 0.09375
- w_time: bfloat16 [256, 1024], P(None, 'dp'), may hold values from -0.375 to 0.375
- gain_attn: bfloat16 [1024], P('dp'), may hold values from 0.5 to 1.5
- gain_mlp: bfloat16 [1024], P('dp'), may hold values from 0.5 to 1.5
- cotangent: bfloat16 [16, 1024, 1024], P('dp'), may hold values from -6 to 6
Outputs:
- block_out: bfloat16 [16, 1024, 1024], P('dp', None, 'tensor')
- input_grad: float32 [16, 1024, 1024], P('dp', None, 'tensor')
- grad_qkv: float32 [3, 1024, 1024], P(None, 'dp', 'tensor')
- grad_out: float32 [1024, 1024], P('tensor', 'dp')
- grad_up: float32 [1024, 4096], P('dp', 'tensor')
- grad_down: float32 [4096, 1024], P('tensor', 'dp')
- grad_time: float32 [256, 1024], P(None, 'dp')
- grad_gain_attn: float32 [1024], P('dp')
- grad_gain_mlp: float32 [1024], P('dp')
Inputs may be any that keep to these rules, and one draw needn't show every extreme that they name: `segment_ids`: in each sequence the ids never fall, every id of 0 to 7 occurs, each document has 1 to 512 tokens and one has exactly 512.
All inputs are finite; a program needn't handle non-finite values.
Results may differ from a plain program's by a relative error of at most 0.022.
Values may be sent and summed in bfloat16 or wider, within the bound.
No kernel may reach another device: no remote copies, remote signals or barrier semaphores. Data moves between devices by JAX's collectives and lax.ppermute only.
A program may use at most 192 MiB of HBM per device.

v0:
```python
import math
import jax
import jax.numpy as jnp
from jax import lax
from jax.sharding import PartitionSpec as P

HEADS = 16
TEMB = 256
eps = 1e-05
masked = -1000000000.0
f32 = jnp.float32
bf16 = jnp.bfloat16


def sinusoid(values, width):
    half = width // 2
    freqs = jnp.exp(-math.log(10000.0) * jnp.arange(half, dtype=f32) / half)
    angles = values[..., None] * freqs
    return jnp.concatenate([jnp.sin(angles), jnp.cos(angles)], axis=-1)


def norm_parts(hidden):
    centre = jnp.mean(hidden, axis=-1, keepdims=True)
    centred = hidden - centre
    spread = jnp.mean(centred * centred, axis=-1, keepdims=True)
    inv = lax.rsqrt(spread + eps)
    return (centred * inv, inv)


def norm_back(unit, inv, gain, grad):
    scaled = grad * gain
    first = jnp.mean(scaled, axis=-1, keepdims=True)
    second = jnp.mean(scaled * unit, axis=-1, keepdims=True)
    return inv * (scaled - first - unit * second)


def positions(segs, offsets):
    seq_len = segs.shape[0]
    index = jnp.arange(seq_len, dtype=jnp.int32)
    member = segs[:, None] == jnp.arange(offsets.shape[0], dtype=jnp.int32)[None, :]
    starts = jnp.min(jnp.where(member, index[:, None], seq_len), axis=0)
    start_tok = jnp.sum(jnp.where(member, starts[None, :], 0), axis=1)
    offset_tok = jnp.sum(jnp.where(member, offsets[None, :], 0), axis=1)
    return offset_tok + index - start_tok


def attend(query, key, value, same, scale):
    scores = jnp.einsum("qhe,khe->hqk", query, key, preferred_element_type=f32) * scale
    scores = jnp.where(same[None], scores, masked)
    top = jnp.max(scores, axis=-1, keepdims=True)
    expo = jnp.exp(scores - top)
    denom = jnp.sum(expo, axis=-1, keepdims=True)
    probs = (expo / denom).astype(bf16)
    out = jnp.einsum("hqk,khe->qhe", probs, value, preferred_element_type=f32)
    return (out, top + jnp.log(denom))


def attend_back(query, key, value, same, scale, lse, d_mixed):
    scores = jnp.einsum("qhe,khe->hqk", query, key, preferred_element_type=f32) * scale
    scores = jnp.where(same[None], scores, masked)
    probs = jnp.exp(scores - lse)
    d_probs = jnp.einsum("qhe,khe->hqk", d_mixed, value, preferred_element_type=f32)
    d_value = jnp.einsum("hqk,qhe->khe", probs.astype(bf16), d_mixed, preferred_element_type=f32)
    delta = jnp.sum(probs * d_probs, axis=-1, keepdims=True)
    d_scores = (probs * (d_probs - delta)).astype(bf16)
    d_query = jnp.einsum("hqk,khe->qhe", d_scores, key, preferred_element_type=f32) * scale
    d_key = jnp.einsum("hqk,qhe->khe", d_scores, query, preferred_element_type=f32) * scale
    return (d_query, d_key, d_value)


def mm(left, right):
    return jnp.dot(left, right, preferred_element_type=f32)


def mm_rt(left, right):
    return jnp.einsum("ik,jk->ij", left, right, preferred_element_type=f32)


def mm_lt(left, right):
    return jnp.einsum("ki,kj->ij", left, right, preferred_element_type=f32)


class Ring:

    def __init__(self, n):
        self.n = n
        self.order = list(range(0, n, 2)) + list(range(n - 1, 0, -2))
        inverse = [self.order.index(i) for i in range(n)]
        self.me = lax.axis_index("dp")
        self.spot = jnp.array(inverse, jnp.int32)[self.me]
        self.table = jnp.array(self.order, jnp.int32)
        self.right = [(self.order[p], self.order[(p + 1) % n]) for p in range(n)]
        self.left = [(b, a) for a, b in self.right]

    def at(self, offset):
        return self.table[(self.spot + offset) % self.n]

    def gather(self, block):
        rows = block.shape[0]
        full = jnp.zeros((self.n * rows,) + block.shape[1:], block.dtype)
        full = lax.dynamic_update_slice_in_dim(full, block, self.me * rows, 0)
        from_left = from_right = block
        for hop in range(1, self.n // 2 + 1):
            from_left = lax.ppermute(from_left, "dp", self.right)
            if hop <= self.n - 1 - self.n // 2:
                from_right = lax.ppermute(from_right, "dp", self.left)
                full = lax.dynamic_update_slice_in_dim(full, from_right, self.at(hop) * rows, 0)
            full = lax.dynamic_update_slice_in_dim(full, from_left, self.at(-hop) * rows, 0)
        return full

    def scatter(self, full):
        rows = full.shape[0] // self.n

        def part(offset):
            return lax.dynamic_slice_in_dim(full, self.at(offset) * rows, rows, 0).astype(f32)

        total = part(0)
        for hops, way, sign in (
            (self.n // 2, self.right, 1),
            (self.n - 1 - self.n // 2, self.left, -1),
        ):
            run = part(sign * hops)
            for hop in range(1, hops + 1):
                run = lax.ppermute(run.astype(bf16), "dp", way).astype(f32)
                if hop < hops:
                    run = run + part(sign * (hops - hop))
            if hops:
                total = total + run
        return total


def swap(value, bit, n):
    return lax.ppermute(value, "tensor", [(i, i ^ bit) for i in range(n)])


def to_features(value, n):
    me = lax.axis_index("tensor")
    tokens, width = value.shape
    value = value.reshape(tokens, n, width // n)
    bit = 1
    while bit < n:
        value = value.reshape(tokens, -1, 2, width // n)
        mine = me // bit % 2
        keep = lax.dynamic_index_in_dim(value, mine, 2, keepdims=False)
        send = lax.dynamic_index_in_dim(value, 1 - mine, 2, keepdims=False)
        got = swap(send.astype(bf16), bit, n).astype(f32)
        if bit == 1:
            got = jnp.concatenate([got[tokens // 2 :], got[: tokens // 2]], axis=0)
        value = keep.astype(f32) + got
        bit *= 2
    return value.reshape(tokens, width // n)


def shards(
    inputs,
    segment_ids,
    doc_offsets,
    time_index,
    w_qkv,
    w_out,
    w_up,
    w_down,
    w_time,
    gain_attn,
    gain_mlp,
    cotangent,
):
    n_dp = lax.axis_size("dp")
    n_tensor = lax.axis_size("tensor")
    me_dp = lax.axis_index("dp")
    core = lax.axis_index("tensor") % 2
    chips = n_tensor // 2
    seqs_dev, seq_len, width = inputs.shape
    half = seq_len // 2
    shard = width // n_tensor
    head_size = width // HEADS
    heads_dev = shard // head_size
    scale = head_size ** (-0.5)
    hidden_dev = w_up.shape[1]
    ring = Ring(n_dp)
    w1_part = jnp.concatenate([w_qkv[0], w_qkv[1], w_qkv[2], w_out.T], axis=1)
    w1 = ring.gather(w1_part)
    w2_part = jnp.concatenate([w_up, w_down.T], axis=1)
    w2 = lax.all_gather(w2_part, "dp", axis=0, tiled=True)
    times = lax.all_gather(time_index, "dp", axis=0, tiled=True)
    temb = sinusoid(times.astype(f32), TEMB)
    cond_part = jnp.dot(temb, w_time.astype(f32), precision=lax.Precision.HIGHEST)
    small = jnp.concatenate(
        [cond_part, gain_attn.astype(f32)[None], gain_mlp.astype(f32)[None]], axis=0
    )
    small = lax.all_gather(small, "dp", axis=1, tiled=True)
    n_seqs = n_dp * seqs_dev
    cond = lax.dynamic_slice_in_dim(small, me_dp * seqs_dev, seqs_dev, 0)
    attn_g, mlp_g = (small[n_seqs], small[n_seqs + 1])

    def own_first(value):
        return jnp.roll(value, -core * half, axis=0)

    def exchange_core(value):
        return swap(value, 1, n_tensor)

    def sum_chips(value):
        bit = 2
        value = value.astype(f32)
        while bit < n_tensor:
            low = value.astype(bf16)
            value = low.astype(f32) + swap(low, bit, n_tensor).astype(f32)
            bit *= 2
        return value

    seqs = range(seqs_dev)
    cot = [own_first(cotangent[i]) for i in seqs]
    segs = [own_first(segment_ids[i]) for i in seqs]
    same = [s[:, None] == s[None, :] for s in segs]
    h0, unit0, inv0, n1 = ([], [], [], [])
    for i in seqs:
        place = own_first(positions(segment_ids[i], doc_offsets[i]))
        h = own_first(inputs[i]).astype(f32) + sinusoid(place.astype(f32), width) + cond[i][None]
        unit, inv = norm_parts(h)
        h0.append(h)
        unit0.append(unit)
        inv0.append(inv)
        n1.append((unit * attn_g).astype(bf16))
    query, key, value, mixed, lse = ([], [], [], [], [])
    h1, unit1, inv1, n2 = ([], [], [], [])
    for i in seqs:
        qkv = mm(n1[i], w1[:, : 3 * shard]).astype(bf16)
        heads = [
            qkv[:, c * shard : (c + 1) * shard].reshape(seq_len, heads_dev, head_size)
            for c in range(3)
        ]
        out, total = attend(*heads, same[i], scale)
        out = out.reshape(seq_len, shard).astype(bf16)
        send = mm_rt(out[half:], w1[:, 3 * shard :]).astype(bf16)
        keep = mm_rt(out[:half], w1[:, 3 * shard :]).astype(bf16)
        attn = sum_chips(keep.astype(f32) + exchange_core(send).astype(f32))
        h = h0[i][:half] + attn
        unit, inv = norm_parts(h)
        own = (unit * mlp_g).astype(bf16)
        query.append(heads[0])
        key.append(heads[1])
        value.append(heads[2])
        mixed.append(out)
        lse.append(total)
        h1.append(h)
        unit1.append(unit)
        inv1.append(inv)
        n2.append(jnp.concatenate([own, exchange_core(own)], axis=0))
    w_up_full, w_down_t = (w2[:, :hidden_dev], w2[:, hidden_dev:])
    active, d_hidden, d_h1, d_h1_low, block_out = ([], [], [], [], [])
    gain_mlp_sum = jnp.zeros((width,), f32)
    for i in seqs:
        hidden = mm(n2[i], w_up_full)
        d_active = mm(cot[i], w_down_t)
        erf = lax.erf(hidden * 0.5**0.5)
        cdf = 0.5 + 0.5 * erf
        active.append((hidden * cdf).astype(bf16))
        slope = cdf + hidden * jnp.exp(-0.5 * hidden * hidden) * (0.5 / math.pi) ** 0.5
        d_hidden.append((d_active * slope).astype(bf16))
        d_n2_send = mm_rt(d_hidden[i][half:], w_up_full).astype(bf16)
        d_n2_keep = mm_rt(d_hidden[i][:half], w_up_full).astype(bf16)
        d_n2 = sum_chips(d_n2_keep.astype(f32) + exchange_core(d_n2_send).astype(f32))
        gain_mlp_sum = gain_mlp_sum + jnp.sum(d_n2 * unit1[i], axis=0)
        d_h1.append(cot[i][:half].astype(f32) + norm_back(unit1[i], inv1[i], mlp_g, d_n2))
        low = d_h1[i].astype(bf16)
        d_h1_low.append(jnp.concatenate([low, exchange_core(low)], axis=0))
        term = mm_rt(active[i], w_down_t)
        term = jnp.concatenate([term[:half] + h1[i] * (1.0 / chips), term[half:]], axis=0)
        block_out.append(to_features(term.astype(bf16), n_tensor).astype(bf16))
    cot_all = jnp.concatenate(cot, axis=0)
    grad2 = jnp.concatenate(
        [
            mm_lt(jnp.concatenate(n2, axis=0), jnp.concatenate(d_hidden, axis=0)).astype(bf16),
            mm_lt(cot_all, jnp.concatenate(active, axis=0)).astype(bf16),
        ],
        axis=1,
    )
    share2 = lax.psum_scatter(grad2, "dp", scatter_dimension=0, tiled=True).astype(f32)
    d_qkv, input_grad, seq_sums = ([], [], [])
    gain_attn_sum = jnp.zeros((width,), f32)
    for i in seqs:
        d_mixed = mm(d_h1_low[i], w1[:, 3 * shard :]).astype(bf16)
        parts = attend_back(
            query[i],
            key[i],
            value[i],
            same[i],
            scale,
            lse[i],
            d_mixed.reshape(seq_len, heads_dev, head_size),
        )
        d_qkv.append(
            jnp.concatenate([p.reshape(seq_len, shard).astype(bf16) for p in parts], axis=1)
        )
        d_n1 = mm_rt(d_qkv[i], w1[:, : 3 * shard])
        gain_attn_sum = gain_attn_sum + jnp.sum(d_n1 * unit0[i], axis=0)
        term = norm_back(unit0[i], inv0[i], attn_g, d_n1)
        term = jnp.concatenate([term[:half] + d_h1[i] * (1.0 / chips), term[half:]], axis=0)
        seq_sums.append(jnp.sum(term, axis=0))
        input_grad.append(to_features(term.astype(bf16), n_tensor))
    grad1 = jnp.concatenate(
        [
            mm_lt(jnp.concatenate(n1, axis=0), jnp.concatenate(d_qkv, axis=0)).astype(bf16),
            mm_lt(jnp.concatenate(d_h1_low, axis=0), jnp.concatenate(mixed, axis=0)).astype(bf16),
        ],
        axis=1,
    )
    share1 = ring.scatter(grad1)
    sums = jnp.zeros((n_seqs, width), f32)
    sums = lax.dynamic_update_slice_in_dim(sums, jnp.stack(seq_sums), me_dp * seqs_dev, 0)
    sums = jnp.concatenate([sums, gain_attn_sum[None], gain_mlp_sum[None] * (1.0 / chips)], axis=0)
    sums = lax.psum(sums, ("dp", "tensor"))
    rows = width // n_dp
    sums = lax.dynamic_slice_in_dim(sums, me_dp * rows, rows, 1)
    factor = float(n_seqs * seq_len) ** (-0.5)
    grad_time = (
        jnp.einsum("st,sd->td", temb, sums[:n_seqs], precision=lax.Precision.HIGHEST) * factor
    )

    def natural(value):
        return jnp.roll(value, core * half, axis=0)

    share1, share2 = (share1 * factor, share2 * factor)
    return (
        jnp.stack([natural(b) for b in block_out]),
        jnp.stack([natural(g) for g in input_grad]),
        jnp.stack([share1[:, c * shard : (c + 1) * shard] for c in range(3)]),
        share1[:, 3 * shard :].T,
        share2[:, :hidden_dev],
        share2[:, hidden_dev:].T,
        grad_time,
        sums[n_seqs] * factor,
        sums[n_seqs + 1] * factor,
    )


def solution(mesh):
    in_specs = (
        P("dp", None, None),
        P("dp", None),
        P("dp", None),
        P("dp"),
        P(None, "dp", "tensor"),
        P("tensor", "dp"),
        P("dp", "tensor"),
        P("tensor", "dp"),
        P(None, "dp"),
        P("dp"),
        P("dp"),
        P("dp", None, None),
    )
    out_specs = (
        P("dp", None, "tensor"),
        P("dp", None, "tensor"),
        P(None, "dp", "tensor"),
        P("tensor", "dp"),
        P("dp", "tensor"),
        P("tensor", "dp"),
        P(None, "dp"),
        P("dp"),
        P("dp"),
    )
    return jax.shard_map(shards, mesh=mesh, in_specs=in_specs, out_specs=out_specs, check_vma=False)
```

profile of v0, /device:TPU:0, one launch (start us, length us, event | category | flops | bytes accessed | tf_op | source)
XLA Modules:
  0.0 683.9 jit_solution(16655282718602888327)
XLA Ops:
  14.9 12.1 %all-reduce = s32[16]{0:T(128)S(1)} all-reduce(s32[16]{0:T(128)S(1)} %dynamic-update-slice), channel_id=1, replica_groups=mesh['dp'=8,'tensor'=4] {'dp'}, use_global_device_ids=true, to_apply=%add | all-reduce | flops 16 | bytes 128
  28.4 31.2 %all_gather.10 = f32[18,1024]{1,0:T(8,128)S(1)} all-gather(f32[18,128]{1,0:T(8,128)S(1)} %pad_maximum_fusion.10), channel_id=1, replica_groups=mesh['dp'=8,'tensor'=4] {'dp'}, dimensions={1}, use_global_device_ids=true | all-gather | bytes 82944 | tf_op jit(solution)/shard_map/all_gather | solution.py:191
  59.7 4.7 slice_bitcast_fusion.3
  64.4 16.2 %multiply_sine_fusion.1 = (f32[1024,512]{1,0:T(8,128)S(1)}, f32[1024,512]{1,0:T(8,128)S(1)}, f32[1024,512]{1,0:T(8,128)}, f32[1024,512]{1,0:T(8,128)}) fusion(f32[512]{0:T(512)S(1)} %multiply_exponential_fusion, f32[1024]{0:T(1024)S(1)} %get-tuple-element.168, f32[1024]{0:T(1024)S(1)} %get-tuple-element.166), kind=kLoop, calls=%fused_computation.119 | loop fusion | flops 1048576 | bytes 8398848 | tf_op jit(solution)/shard_map/sin | solution.py:19
  111.0 4.9 collective-permute-done.6
  118.0 7.5 %fusion.238 = (f32[4,1024]{1,0:T(4,128)S(1)}, f32[4,1024,1024]{1,2,0:T(8,128)}) fusion(bf16[1024,4,64]{0,2,1:T(8,128)(2,1)S(1)} %bitcast.178, bf16[1024,4,64]{0,2,1:T(8,128)(2,1)S(1)} %bitcast.176, pred[1024,1024]{0,1:T(8,128)(4,1)S(1)} %broadcast_compare_fusion.1), kind=kOutput, calls=%fused_computation.439 | convolution fusion | flops 549449728 | bytes 18890752 | tf_op jit(solution)/shard_map/qhe,khe->hqk/dot_general | solution.py:48
  125.5 8.0 %fusion = f32[4,1024]{1,0:T(4,128)S(1)} fusion(f32[4,1024,1024]{1,2,0:T(8,128)} %get-tuple-element.152, f32[4,1024]{1,0:T(4,128)S(1)} %get-tuple-element.151), kind=kLoop, calls=%fused_computation.12 | loop fusion | flops 8384512 | bytes 16809984 | tf_op jit(solution)/shard_map/reduce_sum | solution.py:52
  133.5 7.6 %fusion.144 = bf16[4,64,1024]{2,1,0:T(8,128)(2,1)S(1)} fusion(bf16[1024,4,64]{0,2,1:T(8,128)(2,1)S(1)} %bitcast.188, f32[4,1024,1024]{1,2,0:T(8,128)} %get-tuple-element.152, f32[4,1024]{1,0:T(4,128)S(1)} %fusion, f32[4,1024]{1,0:T(4,128)S(1)} %get-tuple-element.151), kind=kOutput, calls=%fused_computation.250 | convolution fusion | flops 549715968 | bytes 17858560 | tf_op jit(solution)/shard_map/hqk,khe->qhe/dot_general | solution.py:54
  146.3 23.7 %collective-permute-done.8 = bf16[512,1024]{1,0:T(8,128)(2,1)S(1)} collective-permute-done((bf16[512,1024]{1,0:T(8,128)(2,1)S(1)}, bf16[512,1024]{1,0:T(8,128)(2,1)S(1)}, u32[]{:S(2)}, u32[]{:S(2)}) %collective-permute-start.8) | collective-permute-done | bytes 1048608 | tf_op jit(solution)/shard_map/ppermute | solution.py:133
  178.9 4.7 multiply_convert_fusion.4
  206.0 12.1 %collective-permute-done.18 = bf16[512,1024]{1,0:T(8,128)(2,1)} collective-permute-done((bf16[512,1024]{1,0:T(8,128)(2,1)S(1)}, bf16[512,1024]{1,0:T(8,128)(2,1)}, u32[]{:S(2)}, u32[]{:S(2)}) %collective-permute-start.18) | collective-permute-done | bytes 1048608 | tf_op jit(solution)/shard_map/ppermute | solution.py:133
  229.7 9.4 %fusion.124 = bf16[4,64,1024]{2,1,0:T(8,128)(2,1)} fusion(bf16[1024,4,64]{0,2,1:T(8,128)(2,1)S(1)} %bitcast.182, f32[4,1024,1024]{1,2,0:T(8,128)} %get-tuple-element.152, f32[4,1024]{1,0:T(4,128)S(1)} %log_add_fusion.1), kind=kOutput, calls=%fused_computation.240 | convolution fusion | flops 545521664 | bytes 17842176 | tf_op jit(solution)/shard_map/hqk,qhe->khe/dot_general | solution.py:63
  239.1 7.6 %multiply_reduce_fusion.1 = (f32[4,1024]{1,0:T(4,128)S(1)}, f32[4,1024,1024]{1,2,0:T(8,128)}) fusion(f32[4,1024,1024]{1,2,0:T(8,128)S(1)} %bitcast.171, f32[4,1024]{1,0:T(4,128)S(1)} %log_add_fusion.1, bf16[1024,4,64]{0,2,1:T(8,128)(2,1)S(1)} %bitcast.183, bf16[1024,4,64]{0,2,1:T(8,128)(2,1)S(1)} %bitcast.189), kind=kOutput, calls=%fused_computation.4 | convolution fusion | flops 549449728 | bytes 34635776 | tf_op jit(solution)/shard_map/qhe,khe->hqk/dot_general | solution.py:62
  246.7 8.3 %multiply_convert_fusion.1 = bf16[4,1024,1024]{1,2,0:T(8,128)(2,1)S(1)} fusion(f32[4,1024,1024]{1,2,0:T(8,128)} %get-tuple-element.156, f32[4,1024,1024]{1,2,0:T(8,128)S(1)} %bitcast.171, f32[4,1024]{1,0:T(4,128)S(1)} %get-tuple-element.155, f32[4,1024]{1,0:T(4,128)S(1)} %log_add_fusion.1), kind=kLoop, calls=%fused_computation.3 | loop fusion | flops 16777216 | bytes 41975808 | tf_op jit(solution)/shard_map/convert_element_type | solution.py:65
  270.1 7.5 %fusion.239 = (f32[4,1024]{1,0:T(4,128)S(1)}, f32[4,1024,1024]{1,2,0:T(8,128)}) fusion(bf16[1024,4,64]{0,2,1:T(8,128)(2,1)S(1)} %bitcast.174, bf16[1024,4,64]{0,2,1:T(8,128)(2,1)S(1)} %bitcast.172, pred[1024,1024]{0,1:T(8,128)(4,1)S(1)} %broadcast_compare_fusion), kind=kOutput, calls=%fused_computation.440 | convolution fusion | flops 549449728 | bytes 18890752 | tf_op jit(solution)/shard_map/qhe,khe->hqk/dot_general | solution.py:48
  277.5 8.0 %fusion.1 = f32[4,1024]{1,0:T(4,128)S(1)} fusion(f32[4,1024,1024]{1,2,0:T(8,128)} %get-tuple-element.159, f32[4,1024]{1,0:T(4,128)S(1)} %get-tuple-element.158), kind=kLoop, calls=%fused_computation.13 | loop fusion | flops 8384512 | bytes 16809984 | tf_op jit(solution)/shard_map/reduce_sum | solution.py:52
  285.6 7.7 %fusion.143 = bf16[4,64,1024]{2,1,0:T(8,128)(2,1)S(1)} fusion(bf16[1024,4,64]{0,2,1:T(8,128)(2,1)S(1)} %bitcast.186, f32[4,1024,1024]{1,2,0:T(8,128)} %get-tuple-element.159, f32[4,1024]{1,0:T(4,128)S(1)} %fusion.1, f32[4,1024]{1,0:T(4,128)S(1)} %get-tuple-element.158), kind=kOutput, calls=%fused_computation.249 | convolution fusion | flops 549715968 | bytes 17858560 | tf_op jit(solution)/shard_map/hqk,khe->qhe/dot_general | solution.py:54
  298.5 23.7 %collective-permute-done.13 = bf16[512,1024]{1,0:T(8,128)(2,1)S(1)} collective-permute-done((bf16[512,1024]{1,0:T(8,128)(2,1)S(1)}, bf16[512,1024]{1,0:T(8,128)(2,1)S(1)}, u32[]{:S(2)}, u32[]{:S(2)}) %collective-permute-start.13) | collective-permute-done | bytes 1048608 | tf_op jit(solution)/shard_map/ppermute | solution.py:133
  324.3 4.7 fusion.67
  340.2 5.5 multiply_convert_fusion.2
  380.8 9.4 %fusion.89 = bf16[1024,1024]{0,1:T(8,128)(2,1)} fusion(bf16[1024,1024]{1,0:T(8,128)(2,1)} %get-tuple-element.160, bf16[1024,1024]{1,0:T(8,128)(2,1)} %copy-done.109, bf16[1024,1024]{1,0:T(8,128)(2,1)} %fusion.67, bf16[1024,1024]{1,0:T(8,128)(2,1)} %fusion.68), kind=kOutput, calls=%fused_computation.203 | convolution fusion | flops 4312793088 | bytes 10485760 | tf_op jit(solution)/shard_map/ki,kj->ij/dot_general | solution.py:80
  390.2 5.9 collective-permute-done.23
  398.6 4.4 fusion.220
  403.2 9.2 %fusion.94 = bf16[1024,1024]{0,1:T(8,128)(2,1)} fusion(bf16[1024,1024]{1,0:T(8,128)(2,1)} %copy-done.108, bf16[1024,1024]{1,0:T(8,128)(2,1)} %copy-done.107, bf16[512,1024]{1,0:T(8,128)(2,1)} %collective-permute-done.14, bf16[512,1024]{1,0:T(8,128)(2,1)} %multiply_convert_fusion.6, bf16[512,1024]{1,0:T(8,128)(2,1)} %collective-permute-done.9, ...), kind=kOutput, calls=%fused_computation.204 | convolution fusion | flops 4321181696 | bytes 10485760 | tf_op jit(solution)/shard_map/ki,kj->ij/dot_general | solution.py:80
  419.0 10.5 %multiply_reduce_fusion = (f32[4,1024]{1,0:T(4,128)S(1)}, f32[4,1024,1024]{1,2,0:T(8,128)}) fusion(f32[4,1024,1024]{1,2,0:T(8,128)S(1)} %bitcast.169, f32[4,1024]{1,0:T(4,128)S(1)} %log_add_fusion, bf16[1024,4,64]{0,2,1:T(8,128)(2,1)} %bitcast.185, bf16[1024,4,64]{0,2,1:T(8,128)(2,1)} %bitcast.187), kind=kOutput, calls=%fused_computation.1 | convolution fusion | flops 549449728 | bytes 34635776 | tf_op jit(solution)/shard_map/qhe,khe->hqk/dot_general | solution.py:62
  429.6 8.0 %multiply_convert_fusion = bf16[4,1024,1024]{1,2,0:T(8,128)(2,1)S(1)} fusion(f32[4,1024,1024]{1,2,0:T(8,128)} %get-tuple-element.163, f32[4,1024,1024]{1,2,0:T(8,128)S(1)} %bitcast.169, f32[4,1024]{1,0:T(4,128)S(1)} %get-tuple-element.162, f32[4,1024]{1,0:T(4,128)S(1)} %log_add_fusion), kind=kLoop, calls=%fused_computation | loop fusion | flops 16777216 | bytes 41975808 | tf_op jit(solution)/shard_map/convert_element_type | solution.py:65
  454.6 6.7 copy.139
  483.2 7.7 %collective-permute-done.21 = bf16[1024,1,256]{2,0,1:T(8,128)(2,1)} collective-permute-done((bf16[1024,1,256]{2,0,1:T(8,128)(2,1)}, bf16[1024,1,256]{2,0,1:T(8,128)(2,1)}, u32[]{:S(2)}, u32[]{:S(2)}) %collective-permute-start.21) | collective-permute-done | bytes 524320 | tf_op jit(solution)/shard_map/ppermute | solution.py:133
  520.4 49.7 %all-reduce.3.cloned.1.call-done = f32[18,1024]{1,0:T(8,128)} async-done(((f32[18,1024]{1,0:T(8,128)}), f32[18,1024]{1,0:T(8,128)}) %all-reduce.3.cloned.1.call-update) | async-done | bytes 73744 | tf_op jit(solution)/shard_map/psum | solution.py:312
  585.8 14.7 %collective-permute-done.32 = bf16[128,1024]{0,1:T(8,128)(2,1)S(1)} collective-permute-done((bf16[128,1024]{0,1:T(8,128)(2,1)S(1)}, bf16[128,1024]{0,1:T(8,128)(2,1)S(1)}, u32[]{:S(2)}, u32[]{:S(2)}) %collective-permute-start.32) | collective-permute-done | bytes 262176 | tf_op jit(solution)/shard_map/ppermute | solution.py:124
  604.5 16.3 %collective-permute-done.33 = bf16[128,1024]{0,1:T(8,128)(2,1)S(1)} collective-permute-done((bf16[128,1024]{0,1:T(8,128)(2,1)S(1)}, bf16[128,1024]{0,1:T(8,128)(2,1)S(1)}, u32[]{:S(2)}, u32[]{:S(2)}) %collective-permute-start.33) | collective-permute-done | bytes 262176 | tf_op jit(solution)/shard_map/ppermute | solution.py:124
  625.9 47.9 %reduce-scatter.4.cloned.1.call-done = bf16[128,2048]{1,0:T(8,128)(2,1)} async-done(((bf16[1024,2048]{1,0:T(8,128)(2,1)}), bf16[128,2048]{1,0:T(8,128)(2,1)}) %reduce-scatter.4.cloned.1.call-update) | async-done | bytes 524304
  (487 shorter events, 248.7 us)
Async XLA Ops:
  7.2 171.6 %all-gather.2.cloned.1.call-start = ((), (), s32[]{:S(2)}) async-start(), calls=%async_computation.1 | async-start | bytes 4718592 | tf_op jit(solution)/shard_map/all_gather | solution.py:184
  9.1 77.5 %collective-permute-start = (bf16[128,1024]{0,1:T(8,128)(2,1)S(1)}, bf16[128,1024]{0,1:T(8,128)(2,1)}, u32[]{:S(2)}, u32[]{:S(2)}) collective-permute-start(bf16[128,1024]{0,1:T(8,128)(2,1)S(1)} %get-tuple-element.117), channel_id=1, source_target_pairs={{8,0},{16,8},{24,16},{28,24},{20,28},{12,20},{4,12},{0,4},{9,1},{1... | collective-permute-start | bytes 786440 | tf_op jit(solution)/shard_map/ppermute | solution.py:106
  12.1 74.6 %collective-permute-start.1 = (bf16[128,1024]{0,1:T(8,128)(2,1)S(1)}, bf16[128,1024]{0,1:T(8,128)(2,1)S(1)}, u32[]{:S(2)}, u32[]{:S(2)}) collective-permute-start(bf16[128,1024]{0,1:T(8,128)(2,1)S(1)} %get-tuple-element.117), channel_id=1, source_target_pairs={{0,8},{8,16},{16,24},{24,28},{28,20},{20,12},{12,4},{4,0},{1,9},{9... | collective-permute-start | bytes 786440 | tf_op jit(solution)/shard_map/ppermute | solution.py:104
  13.3 556.8 %all-reduce.3.cloned.1.call-start = ((), (), s32[]{:S(2)}) async-start(), calls=%async_computation.2 | async-start | bytes 196608 | tf_op jit(solution)/shard_map/psum | solution.py:312
  86.6 17.2 %collective-permute-start.2 = (bf16[128,1024]{0,1:T(8,128)(2,1)}, bf16[128,1024]{0,1:T(8,128)(2,1)}, u32[]{:S(2)}, u32[]{:S(2)}) collective-permute-start(bf16[128,1024]{0,1:T(8,128)(2,1)} %collective-permute-done), channel_id=1, source_target_pairs={{8,0},{16,8},{24,16},{28,24},{20,28},{12,20},{4,12},{0,4},{9,1},{1... | collective-permute-start | bytes 786440 | tf_op jit(solution)/shard_map/ppermute | solution.py:106
  86.6 15.7 %collective-permute-start.3 = (bf16[128,1024]{0,1:T(8,128)(2,1)S(1)}, bf16[128,1024]{0,1:T(8,128)(2,1)}, u32[]{:S(2)}, u32[]{:S(2)}) collective-permute-start(bf16[128,1024]{0,1:T(8,128)(2,1)S(1)} %collective-permute-done.1), channel_id=1, source_target_pairs={{0,8},{8,16},{16,24},{24,28},{28,20},{20,12},{12,4},{4,0},{1,9},{9... | collective-permute-start | bytes 786440 | tf_op jit(solution)/shard_map/ppermute | solution.py:104
  103.8 6.9 %collective-permute-start.4 = (bf16[128,1024]{0,1:T(8,128)(2,1)}, bf16[128,1024]{0,1:T(8,128)(2,1)S(1)}, u32[]{:S(2)}, u32[]{:S(2)}) collective-permute-start(bf16[128,1024]{0,1:T(8,128)(2,1)} %collective-permute-done.2), channel_id=1, source_target_pairs={{8,0},{16,8},{24,16},{28,24},{20,28},{12,20},{4,12},{0,4},{9,1},{1... | collective-permute-start | bytes 786440 | tf_op jit(solution)/shard_map/ppermute | solution.py:106
  109.0 6.9 %collective-permute-start.6 = (bf16[128,1024]{0,1:T(8,128)(2,1)S(1)}, bf16[128,1024]{0,1:T(8,128)(2,1)S(1)}, u32[]{:S(2)}, u32[]{:S(2)}) collective-permute-start(bf16[128,1024]{0,1:T(8,128)(2,1)S(1)} %collective-permute-done.5), channel_id=1, source_target_pairs={{0,8},{8,16},{16,24},{24,28},{28,20},{20,12},{12,4},{4,0},{1,9},{9... | collective-permute-start | bytes 786440 | tf_op jit(solution)/shard_map/ppermute | solution.py:104
  144.7 25.3 %collective-permute-start.8 = (bf16[512,1024]{1,0:T(8,128)(2,1)S(1)}, bf16[512,1024]{1,0:T(8,128)(2,1)S(1)}, u32[]{:S(2)}, u32[]{:S(2)}) collective-permute-start(bf16[512,1024]{1,0:T(8,128)(2,1)S(1)} %add_convert_fusion.5), channel_id=1, source_target_pairs={{0,2},{1,3},{2,0},{3,1},{4,6},{5,7},{6,4},{7,5},{8,10},{9,11},{10,... | collective-permute-start | bytes 3145736 | tf_op jit(solution)/shard_map/ppermute | solution.py:133
  171.1 7.7 %collective-permute-start.9 = (bf16[512,1024]{1,0:T(8,128)(2,1)S(1)}, bf16[512,1024]{1,0:T(8,128)(2,1)}, u32[]{:S(2)}, u32[]{:S(2)}) collective-permute-start(bf16[512,1024]{1,0:T(8,128)(2,1)S(1)} %multiply_convert_fusion.7), channel_id=1, source_target_pairs={{0,1},{1,0},{2,3},{3,2},{4,5},{5,4},{6,7},{7,6},{8,9},{9,8},{10,11... | collective-permute-start | bytes 3145736 | tf_op jit(solution)/shard_map/ppermute | solution.py:133
  192.7 25.4 %collective-permute-start.18 = (bf16[512,1024]{1,0:T(8,128)(2,1)S(1)}, bf16[512,1024]{1,0:T(8,128)(2,1)}, u32[]{:S(2)}, u32[]{:S(2)}) collective-permute-start(bf16[512,1024]{1,0:T(8,128)(2,1)S(1)} %add_convert_fusion.1), channel_id=1, source_target_pairs={{0,2},{1,3},{2,0},{3,1},{4,6},{5,7},{6,4},{7,5},{8,10},{9,11},{10,... | collective-permute-start | bytes 3145736 | tf_op jit(solution)/shard_map/ppermute | solution.py:133
  296.9 25.3 %collective-permute-start.13 = (bf16[512,1024]{1,0:T(8,128)(2,1)S(1)}, bf16[512,1024]{1,0:T(8,128)(2,1)S(1)}, u32[]{:S(2)}, u32[]{:S(2)}) collective-permute-start(bf16[512,1024]{1,0:T(8,128)(2,1)S(1)} %add_convert_fusion.3), channel_id=1, source_target_pairs={{0,2},{1,3},{2,0},{3,1},{4,6},{5,7},{6,4},{7,5},{8,10},{9,11},{10,... | collective-permute-start | bytes 3145736 | tf_op jit(solution)/shard_map/ppermute | solution.py:133
  324.3 15.6 %collective-permute-start.14 = (bf16[512,1024]{1,0:T(8,128)(2,1)}, bf16[512,1024]{1,0:T(8,128)(2,1)}, u32[]{:S(2)}, u32[]{:S(2)}) collective-permute-start(bf16[512,1024]{1,0:T(8,128)(2,1)} %multiply_convert_fusion.6), channel_id=1, source_target_pairs={{0,1},{1,0},{2,3},{3,2},{4,5},{5,4},{6,7},{7,6},{8,9},{9,8},{10,11... | collective-permute-start | bytes 3145736 | tf_op jit(solution)/shard_map/ppermute | solution.py:133
  339.5 121.9 %collective-permute-start.10 = (bf16[1024,2,256]{2,0,1:T(8,128)(2,1)}, bf16[1024,2,256]{2,0,1:T(8,128)(2,1)}, u32[]{:S(2)}, u32[]{:S(2)}) collective-permute-start(bf16[1024,2,256]{2,0,1:T(8,128)(2,1)} %fusion.154), channel_id=1, source_target_pairs={{0,1},{1,0},{2,3},{3,2},{4,5},{5,4},{6,7},{7,6},{8,9},{9,8},{10,11... | collective-permute-start | bytes 3145736 | tf_op jit(solution)/shard_map/ppermute | solution.py:133
  351.7 14.5 %collective-permute-start.22 = (bf16[512,1024]{1,0:T(8,128)(2,1)}, bf16[512,1024]{1,0:T(8,128)(2,1)}, u32[]{:S(2)}, u32[]{:S(2)}) collective-permute-start(bf16[512,1024]{1,0:T(8,128)(2,1)} %convolution_convert_fusion.2), channel_id=1, source_target_pairs={{0,1},{1,0},{2,3},{3,2},{4,5},{5,4},{6,7},{7,6},{8,9},{9,8},{10,11... | collective-permute-start | bytes 3145736 | tf_op jit(solution)/shard_map/ppermute | solution.py:133
  365.6 100.3 %collective-permute-start.20 = (bf16[1024,2,256]{2,0,1:T(8,128)(2,1)}, bf16[1024,2,256]{2,0,1:T(8,128)(2,1)}, u32[]{:S(2)}, u32[]{:S(2)}) collective-permute-start(bf16[1024,2,256]{2,0,1:T(8,128)(2,1)} %dynamic-slice_bitcast_fusion.1), channel_id=1, source_target_pairs={{0,1},{1,0},{2,3},{3,2},{4,5},{5,4},{6,7},{7,6},{8,9},{9,8},{10,11... | collective-permute-start | bytes 3145736 | tf_op jit(solution)/shard_map/ppermute | solution.py:133
  370.4 25.7 %collective-permute-start.23 = (bf16[512,1024]{1,0:T(8,128)(2,1)}, bf16[512,1024]{1,0:T(8,128)(2,1)}, u32[]{:S(2)}, u32[]{:S(2)}) collective-permute-start(bf16[512,1024]{1,0:T(8,128)(2,1)} %add_convert_fusion), channel_id=1, source_target_pairs={{0,2},{1,3},{2,0},{3,1},{4,6},{5,7},{6,4},{7,5},{8,10},{9,11},{10,... | collective-permute-start | bytes 3145736 | tf_op jit(solution)/shard_map/ppermute | solution.py:133
  403.1 9.3 %collective-permute-start.24 = (bf16[512,1024]{1,0:T(8,128)(2,1)}, bf16[512,1024]{1,0:T(8,128)(2,1)}, u32[]{:S(2)}, u32[]{:S(2)}) collective-permute-start(bf16[512,1024]{1,0:T(8,128)(2,1)} %get-tuple-element.71), channel_id=1, source_target_pairs={{0,1},{1,0},{2,3},{3,2},{4,5},{5,4},{6,7},{7,6},{8,9},{9,8},{10,11... | collective-permute-start | bytes 3145736 | tf_op jit(solution)/shard_map/ppermute | solution.py:133
  450.2 223.6 %reduce-scatter.4.cloned.1.call-start = ((), (), s32[]{:S(2)}) async-start(), calls=%async_computation.3 | async-start | bytes 4718592
  464.4 15.1 %collective-permute-start.11 = (bf16[1024,1,256]{2,0,1:T(8,128)(2,1)}, bf16[1024,1,256]{2,0,1:T(8,128)(2,1)}, u32[]{:S(2)}, u32[]{:S(2)}) collective-permute-start(bf16[1024,1,256]{2,0,1:T(8,128)(2,1)} %dynamic-slice_convert_fusion.3), channel_id=1, source_target_pairs={{0,2},{1,3},{2,0},{3,1},{4,6},{5,7},{6,4},{7,5},{8,10},{9,11},{10,... | collective-permute-start | bytes 1572872 | tf_op jit(solution)/shard_map/ppermute | solution.py:133
  473.2 23.1 %collective-permute-start.15 = (bf16[1024,2,256]{2,0,1:T(8,128)(2,1)}, bf16[1024,2,256]{2,0,1:T(8,128)(2,1)S(1)}, u32[]{:S(2)}, u32[]{:S(2)}) collective-permute-start(bf16[1024,2,256]{2,0,1:T(8,128)(2,1)} %fusion.150), channel_id=1, source_target_pairs={{0,1},{1,0},{2,3},{3,2},{4,5},{5,4},{6,7},{7,6},{8,9},{9,8},{10,11... | collective-permute-start | bytes 3145736 | tf_op jit(solution)/shard_map/ppermute | solution.py:133
  476.0 15.0 %collective-permute-start.21 = (bf16[1024,1,256]{2,0,1:T(8,128)(2,1)}, bf16[1024,1,256]{2,0,1:T(8,128)(2,1)}, u32[]{:S(2)}, u32[]{:S(2)}) collective-permute-start(bf16[1024,1,256]{2,0,1:T(8,128)(2,1)} %dynamic-slice_convert_fusion.1), channel_id=1, source_target_pairs={{0,2},{1,3},{2,0},{3,1},{4,6},{5,7},{6,4},{7,5},{8,10},{9,11},{10,... | collective-permute-start | bytes 1572872 | tf_op jit(solution)/shard_map/ppermute | solution.py:133
  497.7 80.0 %collective-permute-start.16 = (bf16[1024,1,256]{2,0,1:T(8,128)(2,1)}, bf16[1024,1,256]{2,0,1:T(8,128)(2,1)}, u32[]{:S(2)}, u32[]{:S(2)}) collective-permute-start(bf16[1024,1,256]{2,0,1:T(8,128)(2,1)} %dynamic-slice_convert_fusion.2), channel_id=1, source_target_pairs={{0,2},{1,3},{2,0},{3,1},{4,6},{5,7},{6,4},{7,5},{8,10},{9,11},{10,... | collective-permute-start | bytes 1572872 | tf_op jit(solution)/shard_map/ppermute | solution.py:133
  507.4 8.2 %collective-permute-start.27 = (bf16[128,1024]{0,1:T(8,128)(2,1)}, bf16[128,1024]{0,1:T(8,128)(2,1)}, u32[]{:S(2)}, u32[]{:S(2)}) collective-permute-start(bf16[128,1024]{0,1:T(8,128)(2,1)} %get-tuple-element.89), channel_id=1, source_target_pairs={{0,8},{8,16},{16,24},{24,28},{28,20},{20,12},{12,4},{4,0},{1,9},{9... | collective-permute-start | bytes 786440 | tf_op jit(solution)/shard_map/ppermute | solution.py:124
  507.7 71.2 %collective-permute-start.31 = (bf16[128,1024]{0,1:T(8,128)(2,1)}, bf16[128,1024]{0,1:T(8,128)(2,1)S(1)}, u32[]{:S(2)}, u32[]{:S(2)}) collective-permute-start(bf16[128,1024]{0,1:T(8,128)(2,1)} %get-tuple-element.90), channel_id=1, source_target_pairs={{8,0},{16,8},{24,16},{28,24},{20,28},{12,20},{4,12},{0,4},{9,1},{1... | collective-permute-start | bytes 786440 | tf_op jit(solution)/shard_map/ppermute | solution.py:124
  517.4 54.6 %collective-permute-start.28 = (bf16[128,1024]{0,1:T(8,128)(2,1)}, bf16[128,1024]{0,1:T(8,128)(2,1)}, u32[]{:S(2)}, u32[]{:S(2)}) collective-permute-start(bf16[128,1024]{0,1:T(8,128)(2,1)} %add_convert_fusion.12), channel_id=1, source_target_pairs={{0,8},{8,16},{16,24},{24,28},{28,20},{20,12},{12,4},{4,0},{1,9},{9... | collective-permute-start | bytes 786440 | tf_op jit(solution)/shard_map/ppermute | solution.py:124
  520.4 80.2 %collective-permute-start.25 = (bf16[1024,2,256]{2,0,1:T(8,128)(2,1)}, bf16[1024,2,256]{2,0,1:T(8,128)(2,1)S(1)}, u32[]{:S(2)}, u32[]{:S(2)}) collective-permute-start(bf16[1024,2,256]{2,0,1:T(8,128)(2,1)} %dynamic-slice_bitcast_fusion), channel_id=1, source_target_pairs={{0,1},{1,0},{2,3},{3,2},{4,5},{5,4},{6,7},{7,6},{8,9},{9,8},{10,11... | collective-permute-start | bytes 3145736 | tf_op jit(solution)/shard_map/ppermute | solution.py:133
  573.0 7.8 %collective-permute-start.29 = (bf16[128,1024]{0,1:T(8,128)(2,1)S(1)}, bf16[128,1024]{0,1:T(8,128)(2,1)S(1)}, u32[]{:S(2)}, u32[]{:S(2)}) collective-permute-start(bf16[128,1024]{0,1:T(8,128)(2,1)S(1)} %add_convert_fusion.11), channel_id=1, source_target_pairs={{0,8},{8,16},{16,24},{24,28},{28,20},{20,12},{12,4},{4,0},{1,9},{9... | collective-permute-start | bytes 786440 | tf_op jit(solution)/shard_map/ppermute | solution.py:124
  581.0 19.4 %collective-permute-start.32 = (bf16[128,1024]{0,1:T(8,128)(2,1)S(1)}, bf16[128,1024]{0,1:T(8,128)(2,1)S(1)}, u32[]{:S(2)}, u32[]{:S(2)}) collective-permute-start(bf16[128,1024]{0,1:T(8,128)(2,1)S(1)} %get-tuple-element.88), channel_id=1, source_target_pairs={{8,0},{16,8},{24,16},{28,24},{20,28},{12,20},{4,12},{0,4},{9,1},{1... | collective-permute-start | bytes 786440 | tf_op jit(solution)/shard_map/ppermute | solution.py:124
  585.2 19.2 %collective-permute-start.30 = (bf16[128,1024]{0,1:T(8,128)(2,1)S(1)}, bf16[128,1024]{0,1:T(8,128)(2,1)S(1)}, u32[]{:S(2)}, u32[]{:S(2)}) collective-permute-start(bf16[128,1024]{0,1:T(8,128)(2,1)S(1)} %get-tuple-element.87), channel_id=1, source_target_pairs={{0,8},{8,16},{16,24},{24,28},{28,20},{20,12},{12,4},{4,0},{1,9},{9... | collective-permute-start | bytes 786440 | tf_op jit(solution)/shard_map/ppermute | solution.py:124
  600.5 20.2 %collective-permute-start.33 = (bf16[128,1024]{0,1:T(8,128)(2,1)S(1)}, bf16[128,1024]{0,1:T(8,128)(2,1)S(1)}, u32[]{:S(2)}, u32[]{:S(2)}) collective-permute-start(bf16[128,1024]{0,1:T(8,128)(2,1)S(1)} %add_convert_fusion.8), channel_id=1, source_target_pairs={{8,0},{16,8},{24,16},{28,24},{20,28},{12,20},{4,12},{0,4},{9,1},{1... | collective-permute-start | bytes 786440 | tf_op jit(solution)/shard_map/ppermute | solution.py:124
  602.5 20.1 %collective-permute-start.26 = (bf16[1024,1,256]{2,0,1:T(8,128)(2,1)S(1)}, bf16[1024,1,256]{2,0,1:T(8,128)(2,1)S(1)}, u32[]{:S(2)}, u32[]{:S(2)}) collective-permute-start(bf16[1024,1,256]{2,0,1:T(8,128)(2,1)S(1)} %dynamic-slice_convert_fusion), channel_id=1, source_target_pairs={{0,2},{1,3},{2,0},{3,1},{4,6},{5,7},{6,4},{7,5},{8,10},{9,11},{10,... | collective-permute-start | bytes 1572872 | tf_op jit(solution)/shard_map/ppermute | solution.py:133
  (124 other events, 884.6 us)
Sparse Core Ops, SparseCore 0:
  13.4 80.6 all-gather.1
  450.4 119.6 all-reduce.2
  573.7 100.0 reduce-scatter.3
where the time goes:
time: 692 us; the launch traced here: 684 us
  waiting for transfers between devices  223 us (32%)
  matrix products  145 us (21%)
  other arithmetic  122 us (18%)
  local copies, waits for them, and re-layouts  90.8 us (13%)
  blocking collectives  43.3 us (6%)
  starting transfers between devices  30.4 us (4%)
  between operations  29.9 us (4%)
    ppermute x20, waiting for transfers between devices, swap(): return lax.ppermute(value, 'tensor', [(i, i ^ bit) for i in range(n)])  82.7 us
    psum x1, waiting for transfers between devices, shards(): sums = lax.psum(sums, ('dp', 'tensor'))  49.7 us
    unnamed x4, waiting for transfers between devices  47.9 us
    unnamed x253, local copies, waits for them, and re-layouts  38.4 us
    ppermute x7, waiting for transfers between devices, scatter(): run = lax.ppermute(run.astype(bf16), 'dp', way).astype(f32)  35.6 us
    all_gather x1, blocking collectives, shards(): small = lax.all_gather(small, 'dp', axis=1, tiled=True)  31.2 us
    dot_general x8, matrix products, mm(): return jnp.dot(left, right, preferred_element_type=f32)  26.2 us
    dot_general x4, matrix products, mm_lt(): return jnp.einsum('ki,kj->ij', left, right, preferred_element_type=f32)  25 us
  transfers between devices with their start and end apart: 37, of which 18 were waited for; matrix products, arithmetic and copies ran while one was open for 36% of the time, Pallas kernels for 0%

commit v1 on v0

--- a/solution.py
+++ b/solution.py
@@ -188,7 +188,24 @@
     small = jnp.concatenate(
         [cond_part, gain_attn.astype(f32)[None], gain_mlp.astype(f32)[None]], axis=0
     )
-    small = lax.all_gather(small, "dp", axis=1, tiled=True)
+    peers, position, width_2 = (lax.axis_size("dp"), lax.axis_index("dp"), small.shape[1])
+    route = [(i_2, (i_2 + 1) % peers) for i_2 in range(peers)]
+    backward = [(i_2, (i_2 - 1) % peers) for i_2 in range(peers)]
+    result = jnp.zeros((*small.shape[:1], peers * width_2, *small.shape[1 + 1 :]), small.dtype)
+    result = lax.dynamic_update_slice_in_dim(result, small, position * width_2, axis=1)
+    from_left_2 = from_right_2 = small
+    middle = peers // 2
+    for step in range(1, middle + 1):
+        from_left_2 = lax.ppermute(from_left_2, "dp", route)
+        result = lax.dynamic_update_slice_in_dim(
+            result, from_left_2, (position - step) % peers * width_2, axis=1
+        )
+        if step < peers - middle:
+            from_right_2 = lax.ppermute(from_right_2, "dp", backward)
+            result = lax.dynamic_update_slice_in_dim(
+                result, from_right_2, (position + step) % peers * width_2, axis=1
+            )
+    small = result
     n_seqs = n_dp * seqs_dev
     cond = lax.dynamic_slice_in_dim(small, me_dp * seqs_dev, seqs_dev, 0)
     attn_g, mlp_g = (small[n_seqs], small[n_seqs + 1])

time: 692 us -> 711 us (1.027)
  blocking collectives: 43.3 us -> 13.1 us
  waiting for transfers between devices: 223 us -> 242 us
  starting transfers between devices: 30.4 us -> 49.1 us
    all_gather x1 -> x0, blocking collectives: 31.2 us -> none  [shards(): small = lax.all_gather(small, 'dp', axis=1, tiled=True)]
    ppermute x0 -> x7, starting transfers between devices: none -> 14.3 us  [the longest x3 12.7 us: shards(): from_right_2 = lax.ppermute(from_right_2, 'dp', backward)]
    ppermute x0 -> x7, waiting for transfers between devices: none -> 10.5 us  [the longest x4 10.5 us: shards(): from_left_2 = lax.ppermute(from_left_2, 'dp', route)]
    dot_general x12, matrix products: 21.7 us -> 30.2 us  [mm_rt(): return jnp.einsum('ik,jk->ij', left, right, preferred_element_type=f32)]
    ppermute x4, waiting for transfers between devices: 7.25 us -> 15.7 us  [gather(): from_left = lax.ppermute(from_left, 'dp', self.right)]
    unnamed x253 -> x235, local copies, waits for them, and re-layouts: 38.4 us -> 40.7 us
  transfers between devices with their start and end apart: 37 -> 44, of which waited for: 18 -> 22; matrix products, arithmetic and copies ran while one was open for 36% -> 37% of each run, Pallas kernels for 0% -> 0%
where the time goes in v1:
time: 711 us; the launch traced here: 703 us
  waiting for transfers between devices  242 us (34%)
  matrix products  147 us (21%)
  other arithmetic  126 us (18%)
  local copies, waits for them, and re-layouts  96 us (14%)
  starting transfers between devices  49.1 us (7%)
  between operations  29.9 us (4%)
  blocking collectives  13.1 us (2%)
    ppermute x20, waiting for transfers between devices, swap(): return lax.ppermute(value, 'tensor', [(i, i ^ bit) for i in range(n)])  80.8 us
    psum x1, waiting for transfers between devices, shards(): sums = lax.psum(sums, ('dp', 'tensor'))  51.3 us
    unnamed x4, waiting for transfers between devices  47.9 us
    unnamed x235, local copies, waits for them, and re-layouts  40.7 us
    ppermute x7, waiting for transfers between devices, scatter(): run = lax.ppermute(run.astype(bf16), 'dp', way).astype(f32)  35.4 us
    dot_general x12, matrix products, mm_rt(): return jnp.einsum('ik,jk->ij', left, right, preferred_element_type=f32)  30.2 us
    dot_general x8, matrix products, mm(): return jnp.dot(left, right, preferred_element_type=f32)  29.7 us
    dot_general x4, matrix products, mm_lt(): return jnp.einsum('ki,kj->ij', left, right, preferred_element_type=f32)  24.7 us
  transfers between devices with their start and end apart: 44, of which 22 were waited for; matrix products, arithmetic and copies ran while one was open for 37% of the time, Pallas kernels for 0%

profile of v1, /device:TPU:0, one launch (start us, length us, event | category | flops | bytes accessed | tf_op | source)
XLA Modules:
  0.0 703.4 jit_solution(6478496872982605712)
XLA Ops:
  10.1 13.1 %all-reduce = s32[16]{0:T(128)S(1)} all-reduce(s32[16]{0:T(128)S(1)} %dynamic-update-slice), channel_id=1, replica_groups=mesh['dp'=8,'tensor'=4] {'dp'}, use_global_device_ids=true, to_apply=%add | all-reduce | flops 16 | bytes 128
  38.5 4.8 slice_bitcast_fusion.3
  43.3 17.2 %multiply_sine_fusion.1 = (f32[1024,512]{1,0:T(8,128)}, f32[1024,512]{1,0:T(8,128)}, f32[1024,512]{1,0:T(8,128)}, f32[1024,512]{1,0:T(8,128)}) fusion(f32[512]{0:T(512)S(1)} %multiply_exponential_fusion, f32[1024]{0:T(1024)S(1)} %fusion.204, f32[1024]{0:T(1024)S(1)} %fusion.201), kind=kLoop, calls=%fused_computation.119 | loop fusion | flops 1048576 | bytes 8398848 | tf_op jit(solution)/shard_map/sin | solution.py:19
  72.4 4.7 collective-permute-start.3
  79.1 4.8 collective-permute-start.5
  85.6 6.7 collective-permute-done.6
  99.2 11.0 %collective-permute-done.10 = bf16[128,1024]{0,1:T(8,128)(2,1)S(1)} collective-permute-done((bf16[128,1024]{0,1:T(8,128)(2,1)S(1)}, bf16[128,1024]{0,1:T(8,128)(2,1)S(1)}, u32[]{:S(2)}, u32[]{:S(2)}) %collective-permute-start.10) | collective-permute-done | bytes 262176 | tf_op jit(solution)/shard_map/ppermute | solution.py:104
  130.0 7.5 %fusion.238 = (f32[4,1024]{1,0:T(4,128)S(1)}, f32[4,1024,1024]{1,2,0:T(8,128)}) fusion(bf16[1024,4,64]{0,2,1:T(8,128)(2,1)S(1)} %bitcast.178, bf16[1024,4,64]{0,2,1:T(8,128)(2,1)S(1)} %bitcast.176, pred[1024,1024]{0,1:T(8,128)(4,1)S(1)} %broadcast_compare_fusion.1), kind=kOutput, calls=%fused_computation.447 | convolution fusion | flops 549449728 | bytes 18890752 | tf_op jit(solution)/shard_map/qhe,khe->hqk/dot_general | solution.py:48
  137.5 8.0 %fusion = f32[4,1024]{1,0:T(4,128)S(1)} fusion(f32[4,1024,1024]{1,2,0:T(8,128)} %get-tuple-element.154, f32[4,1024]{1,0:T(4,128)S(1)} %get-tuple-element.153), kind=kLoop, calls=%fused_computation.12 | loop fusion | flops 8384512 | bytes 16809984 | tf_op jit(solution)/shard_map/reduce_sum | solution.py:52
  145.5 7.9 %fusion.144 = bf16[4,64,1024]{2,1,0:T(8,128)(2,1)S(1)} fusion(bf16[1024,4,64]{0,2,1:T(8,128)(2,1)S(1)} %bitcast.188, f32[4,1024,1024]{1,2,0:T(8,128)} %get-tuple-element.154, f32[4,1024]{1,0:T(4,128)S(1)} %fusion, f32[4,1024]{1,0:T(4,128)S(1)} %get-tuple-element.153), kind=kOutput, calls=%fused_computation.250 | convolution fusion | flops 549715968 | bytes 17858560 | tf_op jit(solution)/shard_map/hqk,khe->qhe/dot_general | solution.py:54
  159.8 23.7 %collective-permute-done.15 = bf16[512,1024]{1,0:T(8,128)(2,1)S(1)} collective-permute-done((bf16[512,1024]{1,0:T(8,128)(2,1)S(1)}, bf16[512,1024]{1,0:T(8,128)(2,1)S(1)}, u32[]{:S(2)}, u32[]{:S(2)}) %collective-permute-start.15) | collective-permute-done | bytes 1048608 | tf_op jit(solution)/shard_map/ppermute | solution.py:133
  192.5 5.0 multiply_convert_fusion.4
  219.7 13.5 %collective-permute-done.25 = bf16[512,1024]{1,0:T(8,128)(2,1)} collective-permute-done((bf16[512,1024]{1,0:T(8,128)(2,1)}, bf16[512,1024]{1,0:T(8,128)(2,1)}, u32[]{:S(2)}, u32[]{:S(2)}) %collective-permute-start.25) | collective-permute-done | bytes 1048608 | tf_op jit(solution)/shard_map/ppermute | solution.py:133
  252.0 7.8 %multiply_reduce_fusion.1 = (f32[4,1024]{1,0:T(4,128)S(1)}, f32[4,1024,1024]{1,2,0:T(8,128)}) fusion(f32[4,1024,1024]{1,2,0:T(8,128)S(1)} %bitcast.171, f32[4,1024]{1,0:T(4,128)S(1)} %log_add_fusion.1, bf16[1024,4,64]{0,2,1:T(8,128)(2,1)S(1)} %bitcast.183, bf16[1024,4,64]{0,2,1:T(8,128)(2,1)S(1)} %bitcast.189), kind=kOutput, calls=%fused_computation.4 | convolution fusion | flops 549449728 | bytes 34635776 | tf_op jit(solution)/shard_map/qhe,khe->hqk/dot_general | solution.py:62
  259.9 7.9 %multiply_convert_fusion.1 = bf16[4,1024,1024]{1,2,0:T(8,128)(2,1)S(1)} fusion(f32[4,1024,1024]{1,2,0:T(8,128)} %get-tuple-element.158, f32[4,1024,1024]{1,2,0:T(8,128)S(1)} %bitcast.171, f32[4,1024]{1,0:T(4,128)S(1)} %get-tuple-element.157, f32[4,1024]{1,0:T(4,128)S(1)} %log_add_fusion.1), kind=kLoop, calls=%fused_computation.3 | loop fusion | flops 16777216 | bytes 41975808 | tf_op jit(solution)/shard_map/convert_element_type | solution.py:65
  272.8 5.2 multiply_reduce_fusion.3
  287.8 7.8 %fusion.239 = (f32[4,1024]{1,0:T(4,128)S(1)}, f32[4,1024,1024]{1,2,0:T(8,128)}) fusion(bf16[1024,4,64]{0,2,1:T(8,128)(2,1)S(1)} %bitcast.174, bf16[1024,4,64]{0,2,1:T(8,128)(2,1)S(1)} %bitcast.172, pred[1024,1024]{0,1:T(8,128)(4,1)S(1)} %copy-done.9), kind=kOutput, calls=%fused_computation.448 | convolution fusion | flops 549449728 | bytes 18890752 | tf_op jit(solution)/shard_map/qhe,khe->hqk/dot_general | solution.py:48
  295.6 8.0 %fusion.1 = f32[4,1024]{1,0:T(4,128)S(1)} fusion(f32[4,1024,1024]{1,2,0:T(8,128)} %get-tuple-element.161, f32[4,1024]{1,0:T(4,128)S(1)} %get-tuple-element.160), kind=kLoop, calls=%fused_computation.13 | loop fusion | flops 8384512 | bytes 16809984 | tf_op jit(solution)/shard_map/reduce_sum | solution.py:52
  303.6 7.4 %fusion.143 = bf16[4,64,1024]{2,1,0:T(8,128)(2,1)S(1)} fusion(bf16[1024,4,64]{0,2,1:T(8,128)(2,1)S(1)} %bitcast.186, f32[4,1024,1024]{1,2,0:T(8,128)} %get-tuple-element.161, f32[4,1024]{1,0:T(4,128)S(1)} %fusion.1, f32[4,1024]{1,0:T(4,128)S(1)} %get-tuple-element.160), kind=kOutput, calls=%fused_computation.249 | convolution fusion | flops 549715968 | bytes 17858560 | tf_op jit(solution)/shard_map/hqk,khe->qhe/dot_general | solution.py:54
  317.4 23.7 %collective-permute-done.20 = bf16[512,1024]{1,0:T(8,128)(2,1)S(1)} collective-permute-done((bf16[512,1024]{1,0:T(8,128)(2,1)S(1)}, bf16[512,1024]{1,0:T(8,128)(2,1)S(1)}, u32[]{:S(2)}, u32[]{:S(2)}) %collective-permute-start.20) | collective-permute-done | bytes 1048608 | tf_op jit(solution)/shard_map/ppermute | solution.py:133
  359.2 5.5 multiply_convert_fusion.2
  400.0 9.4 %fusion.89 = bf16[1024,1024]{0,1:T(8,128)(2,1)} fusion(bf16[1024,1024]{1,0:T(8,128)(2,1)} %get-tuple-element.162, bf16[1024,1024]{1,0:T(8,128)(2,1)} %copy-done.100, bf16[1024,1024]{1,0:T(8,128)(2,1)} %fusion.67, bf16[1024,1024]{1,0:T(8,128)(2,1)} %fusion.68), kind=kOutput, calls=%fused_computation.203 | convolution fusion | flops 4312793088 | bytes 10485760 | tf_op jit(solution)/shard_map/ki,kj->ij/dot_general | solution.py:80
  409.4 5.6 collective-permute-done.30
  421.7 9.2 %fusion.94 = bf16[1024,1024]{0,1:T(8,128)(2,1)} fusion(bf16[1024,1024]{1,0:T(8,128)(2,1)} %copy-done.99, bf16[1024,1024]{1,0:T(8,128)(2,1)} %copy-done.98, bf16[512,1024]{1,0:T(8,128)(2,1)} %collective-permute-done.21, bf16[512,1024]{1,0:T(8,128)(2,1)} %multiply_convert_fusion.6, bf16[512,1024]{1,0:T(8,128)(2,1)} %collective-permute-done.16, ...), kind=kOutput, calls=%fused_computation.204 | convolution fusion | flops 4321181696 | bytes 10485760 | tf_op jit(solution)/shard_map/ki,kj->ij/dot_general | solution.py:80
  436.7 7.6 %multiply_reduce_fusion = (f32[4,1024]{1,0:T(4,128)S(1)}, f32[4,1024,1024]{1,2,0:T(8,128)}) fusion(f32[4,1024,1024]{1,2,0:T(8,128)S(1)} %bitcast.169, f32[4,1024]{1,0:T(4,128)S(1)} %log_add_fusion, bf16[1024,4,64]{0,2,1:T(8,128)(2,1)S(1)} %bitcast.185, bf16[1024,4,64]{0,2,1:T(8,128)(2,1)S(1)} %bitcast.187), kind=kOutput, calls=%fused_computation.1 | convolution fusion | flops 549449728 | bytes 34635776 | tf_op jit(solution)/shard_map/qhe,khe->hqk/dot_general | solution.py:62
  444.3 7.9 %multiply_convert_fusion = bf16[4,1024,1024]{1,2,0:T(8,128)(2,1)S(1)} fusion(f32[4,1024,1024]{1,2,0:T(8,128)} %get-tuple-element.165, f32[4,1024,1024]{1,2,0:T(8,128)S(1)} %bitcast.169, f32[4,1024]{1,0:T(4,128)S(1)} %get-tuple-element.164, f32[4,1024]{1,0:T(4,128)S(1)} %log_add_fusion), kind=kLoop, calls=%fused_computation | loop fusion | flops 16777216 | bytes 41975808 | tf_op jit(solution)/shard_map/convert_element_type | solution.py:65
  470.5 6.7 copy.139
  499.1 7.6 %collective-permute-done.28 = bf16[1024,1,256]{2,0,1:T(8,128)(2,1)} collective-permute-done((bf16[1024,1,256]{2,0,1:T(8,128)(2,1)}, bf16[1024,1,256]{2,0,1:T(8,128)(2,1)}, u32[]{:S(2)}, u32[]{:S(2)}) %collective-permute-start.28) | collective-permute-done | bytes 524320 | tf_op jit(solution)/shard_map/ppermute | solution.py:133
  538.4 51.3 %all-reduce.3.cloned.1.call-done = f32[18,1024]{1,0:T(8,128)} async-done(((f32[18,1024]{1,0:T(8,128)}), f32[18,1024]{1,0:T(8,128)}) %all-reduce.3.cloned.1.call-update) | async-done | bytes 73744 | tf_op jit(solution)/shard_map/psum | solution.py:329
  605.3 14.7 %collective-permute-done.39 = bf16[128,1024]{0,1:T(8,128)(2,1)S(1)} collective-permute-done((bf16[128,1024]{0,1:T(8,128)(2,1)S(1)}, bf16[128,1024]{0,1:T(8,128)(2,1)S(1)}, u32[]{:S(2)}, u32[]{:S(2)}) %collective-permute-start.39) | collective-permute-done | bytes 262176 | tf_op jit(solution)/shard_map/ppermute | solution.py:124
  624.0 16.4 %collective-permute-done.40 = bf16[128,1024]{0,1:T(8,128)(2,1)S(1)} collective-permute-done((bf16[128,1024]{0,1:T(8,128)(2,1)S(1)}, bf16[128,1024]{0,1:T(8,128)(2,1)S(1)}, u32[]{:S(2)}, u32[]{:S(2)}) %collective-permute-start.40) | collective-permute-done | bytes 262176 | tf_op jit(solution)/shard_map/ppermute | solution.py:124
  645.5 47.9 %reduce-scatter.4.cloned.1.call-done = bf16[128,2048]{1,0:T(8,128)(2,1)} async-done(((bf16[1024,2048]{1,0:T(8,128)(2,1)}), bf16[128,2048]{1,0:T(8,128)(2,1)}) %reduce-scatter.4.cloned.1.call-update) | async-done | bytes 524304
  (490 shorter events, 288.3 us)
Async XLA Ops:
  7.2 185.3 %all-gather.2.cloned.1.call-start = ((), (), s32[]{:S(2)}) async-start(), calls=%async_computation.1 | async-start | bytes 4718592 | tf_op jit(solution)/shard_map/all_gather | solution.py:184
  24.2 48.1 %collective-permute-start = (f32[18,128]{1,0:T(8,128)S(1)}, f32[18,128]{1,0:T(8,128)S(1)}, u32[]{:S(2)}, u32[]{:S(2)}) collective-permute-start(f32[18,128]{1,0:T(8,128)S(1)} %get-tuple-element.128), channel_id=1, source_target_pairs={{0,4},{4,8},{8,12},{12,16},{16,20},{20,24},{24,28},{28,0},{1,5},{5... | collective-permute-start | bytes 27656 | tf_op jit(solution)/shard_map/ppermute | solution.py:199
  25.7 46.6 %collective-permute-start.1 = (f32[18,128]{1,0:T(8,128)S(1)}, f32[18,128]{1,0:T(8,128)S(1)}, u32[]{:S(2)}, u32[]{:S(2)}) collective-permute-start(f32[18,128]{1,0:T(8,128)S(1)} %get-tuple-element.128), channel_id=1, source_target_pairs={{0,28},{4,0},{8,4},{12,8},{16,12},{20,16},{24,20},{28,24},{1,29},{... | collective-permute-start | bytes 27656 | tf_op jit(solution)/shard_map/ppermute | solution.py:204
  32.6 63.9 %collective-permute-start.7 = (bf16[128,1024]{0,1:T(8,128)(2,1)S(1)}, bf16[128,1024]{0,1:T(8,128)(2,1)S(1)}, u32[]{:S(2)}, u32[]{:S(2)}) collective-permute-start(bf16[128,1024]{0,1:T(8,128)(2,1)S(1)} %get-tuple-element.117), channel_id=1, source_target_pairs={{8,0},{16,8},{24,16},{28,24},{20,28},{12,20},{4,12},{0,4},{9,1},{1... | collective-permute-start | bytes 786440 | tf_op jit(solution)/shard_map/ppermute | solution.py:106
  32.6 64.0 %collective-permute-start.8 = (bf16[128,1024]{0,1:T(8,128)(2,1)S(1)}, bf16[128,1024]{0,1:T(8,128)(2,1)S(1)}, u32[]{:S(2)}, u32[]{:S(2)}) collective-permute-start(bf16[128,1024]{0,1:T(8,128)(2,1)S(1)} %get-tuple-element.117), channel_id=1, source_target_pairs={{0,8},{8,16},{16,24},{24,28},{28,20},{20,12},{12,4},{4,0},{1,9},{9... | collective-permute-start | bytes 786440 | tf_op jit(solution)/shard_map/ppermute | solution.py:104
  35.6 554.0 %all-reduce.3.cloned.1.call-start = ((), (), s32[]{:S(2)}) async-start(), calls=%async_computation.2 | async-start | bytes 196608 | tf_op jit(solution)/shard_map/psum | solution.py:329
  96.5 18.0 %collective-permute-start.9 = (bf16[128,1024]{0,1:T(8,128)(2,1)S(1)}, bf16[128,1024]{0,1:T(8,128)(2,1)S(1)}, u32[]{:S(2)}, u32[]{:S(2)}) collective-permute-start(bf16[128,1024]{0,1:T(8,128)(2,1)S(1)} %collective-permute-done.7), channel_id=1, source_target_pairs={{8,0},{16,8},{24,16},{28,24},{20,28},{12,20},{4,12},{0,4},{9,1},{1... | collective-permute-start | bytes 786440 | tf_op jit(solution)/shard_map/ppermute | solution.py:106
  96.6 13.6 %collective-permute-start.10 = (bf16[128,1024]{0,1:T(8,128)(2,1)S(1)}, bf16[128,1024]{0,1:T(8,128)(2,1)S(1)}, u32[]{:S(2)}, u32[]{:S(2)}) collective-permute-start(bf16[128,1024]{0,1:T(8,128)(2,1)S(1)} %collective-permute-done.8), channel_id=1, source_target_pairs={{0,8},{8,16},{16,24},{24,28},{28,20},{20,12},{12,4},{4,0},{1,9},{9... | collective-permute-start | bytes 786440 | tf_op jit(solution)/shard_map/ppermute | solution.py:104
  110.1 9.0 %collective-permute-start.12 = (bf16[128,1024]{0,1:T(8,128)(2,1)S(1)}, bf16[128,1024]{0,1:T(8,128)(2,1)S(1)}, u32[]{:S(2)}, u32[]{:S(2)}) collective-permute-start(bf16[128,1024]{0,1:T(8,128)(2,1)S(1)} %collective-permute-done.10), channel_id=1, source_target_pairs={{0,8},{8,16},{16,24},{24,28},{28,20},{20,12},{12,4},{4,0},{1,9},{9... | collective-permute-start | bytes 786440 | tf_op jit(solution)/shard_map/ppermute | solution.py:104
  114.5 8.3 %collective-permute-start.11 = (bf16[128,1024]{0,1:T(8,128)(2,1)S(1)}, bf16[128,1024]{0,1:T(8,128)(2,1)S(1)}, u32[]{:S(2)}, u32[]{:S(2)}) collective-permute-start(bf16[128,1024]{0,1:T(8,128)(2,1)S(1)} %collective-permute-done.9), channel_id=1, source_target_pairs={{8,0},{16,8},{24,16},{28,24},{20,28},{12,20},{4,12},{0,4},{9,1},{1... | collective-permute-start | bytes 786440 | tf_op jit(solution)/shard_map/ppermute | solution.py:106
  158.3 25.3 %collective-permute-start.15 = (bf16[512,1024]{1,0:T(8,128)(2,1)S(1)}, bf16[512,1024]{1,0:T(8,128)(2,1)S(1)}, u32[]{:S(2)}, u32[]{:S(2)}) collective-permute-start(bf16[512,1024]{1,0:T(8,128)(2,1)S(1)} %add_convert_fusion.5), channel_id=1, source_target_pairs={{0,2},{1,3},{2,0},{3,1},{4,6},{5,7},{6,4},{7,5},{8,10},{9,11},{10,... | collective-permute-start | bytes 3145736 | tf_op jit(solution)/shard_map/ppermute | solution.py:133
  207.8 25.5 %collective-permute-start.25 = (bf16[512,1024]{1,0:T(8,128)(2,1)}, bf16[512,1024]{1,0:T(8,128)(2,1)}, u32[]{:S(2)}, u32[]{:S(2)}) collective-permute-start(bf16[512,1024]{1,0:T(8,128)(2,1)} %add_convert_fusion.1), channel_id=1, source_target_pairs={{0,2},{1,3},{2,0},{3,1},{4,6},{5,7},{6,4},{7,5},{8,10},{9,11},{10,... | collective-permute-start | bytes 3145736 | tf_op jit(solution)/shard_map/ppermute | solution.py:133
  315.9 25.3 %collective-permute-start.20 = (bf16[512,1024]{1,0:T(8,128)(2,1)S(1)}, bf16[512,1024]{1,0:T(8,128)(2,1)S(1)}, u32[]{:S(2)}, u32[]{:S(2)}) collective-permute-start(bf16[512,1024]{1,0:T(8,128)(2,1)S(1)} %add_convert_fusion.3), channel_id=1, source_target_pairs={{0,2},{1,3},{2,0},{3,1},{4,6},{5,7},{6,4},{7,5},{8,10},{9,11},{10,... | collective-permute-start | bytes 3145736 | tf_op jit(solution)/shard_map/ppermute | solution.py:133
  343.3 15.7 %collective-permute-start.21 = (bf16[512,1024]{1,0:T(8,128)(2,1)}, bf16[512,1024]{1,0:T(8,128)(2,1)}, u32[]{:S(2)}, u32[]{:S(2)}) collective-permute-start(bf16[512,1024]{1,0:T(8,128)(2,1)} %multiply_convert_fusion.6), channel_id=1, source_target_pairs={{0,1},{1,0},{2,3},{3,2},{4,5},{5,4},{6,7},{7,6},{8,9},{9,8},{10,11... | collective-permute-start | bytes 3145736 | tf_op jit(solution)/shard_map/ppermute | solution.py:133
  358.5 118.7 %collective-permute-start.17 = (bf16[1024,2,256]{2,0,1:T(8,128)(2,1)}, bf16[1024,2,256]{2,0,1:T(8,128)(2,1)}, u32[]{:S(2)}, u32[]{:S(2)}) collective-permute-start(bf16[1024,2,256]{2,0,1:T(8,128)(2,1)} %fusion.154), channel_id=1, source_target_pairs={{0,1},{1,0},{2,3},{3,2},{4,5},{5,4},{6,7},{7,6},{8,9},{9,8},{10,11... | collective-permute-start | bytes 3145736 | tf_op jit(solution)/shard_map/ppermute | solution.py:133
  370.7 14.3 %collective-permute-start.29 = (bf16[512,1024]{1,0:T(8,128)(2,1)}, bf16[512,1024]{1,0:T(8,128)(2,1)}, u32[]{:S(2)}, u32[]{:S(2)}) collective-permute-start(bf16[512,1024]{1,0:T(8,128)(2,1)} %convolution_convert_fusion.2), channel_id=1, source_target_pairs={{0,1},{1,0},{2,3},{3,2},{4,5},{5,4},{6,7},{7,6},{8,9},{9,8},{10,11... | collective-permute-start | bytes 3145736 | tf_op jit(solution)/shard_map/ppermute | solution.py:133
  384.5 97.2 %collective-permute-start.27 = (bf16[1024,2,256]{2,0,1:T(8,128)(2,1)}, bf16[1024,2,256]{2,0,1:T(8,128)(2,1)}, u32[]{:S(2)}, u32[]{:S(2)}) collective-permute-start(bf16[1024,2,256]{2,0,1:T(8,128)(2,1)} %dynamic-slice_bitcast_fusion.1), channel_id=1, source_target_pairs={{0,1},{1,0},{2,3},{3,2},{4,5},{5,4},{6,7},{7,6},{8,9},{9,8},{10,11... | collective-permute-start | bytes 3145736 | tf_op jit(solution)/shard_map/ppermute | solution.py:133
  389.3 25.7 %collective-permute-start.30 = (bf16[512,1024]{1,0:T(8,128)(2,1)}, bf16[512,1024]{1,0:T(8,128)(2,1)}, u32[]{:S(2)}, u32[]{:S(2)}) collective-permute-start(bf16[512,1024]{1,0:T(8,128)(2,1)} %add_convert_fusion), channel_id=1, source_target_pairs={{0,2},{1,3},{2,0},{3,1},{4,6},{5,7},{6,4},{7,5},{8,10},{9,11},{10,... | collective-permute-start | bytes 3145736 | tf_op jit(solution)/shard_map/ppermute | solution.py:133
  421.6 9.3 %collective-permute-start.31 = (bf16[512,1024]{1,0:T(8,128)(2,1)}, bf16[512,1024]{1,0:T(8,128)(2,1)S(1)}, u32[]{:S(2)}, u32[]{:S(2)}) collective-permute-start(bf16[512,1024]{1,0:T(8,128)(2,1)} %get-tuple-element.71), channel_id=1, source_target_pairs={{0,1},{1,0},{2,3},{3,2},{4,5},{5,4},{6,7},{7,6},{8,9},{9,8},{10,11... | collective-permute-start | bytes 3145736 | tf_op jit(solution)/shard_map/ppermute | solution.py:133
  466.1 227.2 %reduce-scatter.4.cloned.1.call-start = ((), (), s32[]{:S(2)}) async-start(), calls=%async_computation.3 | async-start | bytes 4718592
  480.2 15.2 %collective-permute-start.18 = (bf16[1024,1,256]{2,0,1:T(8,128)(2,1)}, bf16[1024,1,256]{2,0,1:T(8,128)(2,1)}, u32[]{:S(2)}, u32[]{:S(2)}) collective-permute-start(bf16[1024,1,256]{2,0,1:T(8,128)(2,1)} %dynamic-slice_convert_fusion.3), channel_id=1, source_target_pairs={{0,2},{1,3},{2,0},{3,1},{4,6},{5,7},{6,4},{7,5},{8,10},{9,11},{10,... | collective-permute-start | bytes 1572872 | tf_op jit(solution)/shard_map/ppermute | solution.py:133
  489.0 23.1 %collective-permute-start.22 = (bf16[1024,2,256]{2,0,1:T(8,128)(2,1)}, bf16[1024,2,256]{2,0,1:T(8,128)(2,1)S(1)}, u32[]{:S(2)}, u32[]{:S(2)}) collective-permute-start(bf16[1024,2,256]{2,0,1:T(8,128)(2,1)} %fusion.150), channel_id=1, source_target_pairs={{0,1},{1,0},{2,3},{3,2},{4,5},{5,4},{6,7},{7,6},{8,9},{9,8},{10,11... | collective-permute-start | bytes 3145736 | tf_op jit(solution)/shard_map/ppermute | solution.py:133
  491.6 15.1 %collective-permute-start.28 = (bf16[1024,1,256]{2,0,1:T(8,128)(2,1)}, bf16[1024,1,256]{2,0,1:T(8,128)(2,1)}, u32[]{:S(2)}, u32[]{:S(2)}) collective-permute-start(bf16[1024,1,256]{2,0,1:T(8,128)(2,1)} %dynamic-slice_convert_fusion.1), channel_id=1, source_target_pairs={{0,2},{1,3},{2,0},{3,1},{4,6},{5,7},{6,4},{7,5},{8,10},{9,11},{10,... | collective-permute-start | bytes 1572872 | tf_op jit(solution)/shard_map/ppermute | solution.py:133
  513.4 83.8 %collective-permute-start.23 = (bf16[1024,1,256]{2,0,1:T(8,128)(2,1)}, bf16[1024,1,256]{2,0,1:T(8,128)(2,1)}, u32[]{:S(2)}, u32[]{:S(2)}) collective-permute-start(bf16[1024,1,256]{2,0,1:T(8,128)(2,1)} %dynamic-slice_convert_fusion.2), channel_id=1, source_target_pairs={{0,2},{1,3},{2,0},{3,1},{4,6},{5,7},{6,4},{7,5},{8,10},{9,11},{10,... | collective-permute-start | bytes 1572872 | tf_op jit(solution)/shard_map/ppermute | solution.py:133
  523.2 8.4 %collective-permute-start.34 = (bf16[128,1024]{0,1:T(8,128)(2,1)}, bf16[128,1024]{0,1:T(8,128)(2,1)}, u32[]{:S(2)}, u32[]{:S(2)}) collective-permute-start(bf16[128,1024]{0,1:T(8,128)(2,1)} %get-tuple-element.89), channel_id=1, source_target_pairs={{0,8},{8,16},{16,24},{24,28},{28,20},{20,12},{12,4},{4,0},{1,9},{9... | collective-permute-start | bytes 786440 | tf_op jit(solution)/shard_map/ppermute | solution.py:124
  525.6 72.8 %collective-permute-start.38 = (bf16[128,1024]{0,1:T(8,128)(2,1)}, bf16[128,1024]{0,1:T(8,128)(2,1)S(1)}, u32[]{:S(2)}, u32[]{:S(2)}) collective-permute-start(bf16[128,1024]{0,1:T(8,128)(2,1)} %get-tuple-element.90), channel_id=1, source_target_pairs={{8,0},{16,8},{24,16},{28,24},{20,28},{12,20},{4,12},{0,4},{9,1},{1... | collective-permute-start | bytes 786440 | tf_op jit(solution)/shard_map/ppermute | solution.py:124
  533.3 58.3 %collective-permute-start.35 = (bf16[128,1024]{0,1:T(8,128)(2,1)}, bf16[128,1024]{0,1:T(8,128)(2,1)}, u32[]{:S(2)}, u32[]{:S(2)}) collective-permute-start(bf16[128,1024]{0,1:T(8,128)(2,1)} %add_convert_fusion.12), channel_id=1, source_target_pairs={{0,8},{8,16},{16,24},{24,28},{28,20},{20,12},{12,4},{4,0},{1,9},{9... | collective-permute-start | bytes 786440 | tf_op jit(solution)/shard_map/ppermute | solution.py:124
  538.4 81.8 %collective-permute-start.32 = (bf16[1024,2,256]{2,0,1:T(8,128)(2,1)}, bf16[1024,2,256]{2,0,1:T(8,128)(2,1)S(1)}, u32[]{:S(2)}, u32[]{:S(2)}) collective-permute-start(bf16[1024,2,256]{2,0,1:T(8,128)(2,1)} %dynamic-slice_bitcast_fusion), channel_id=1, source_target_pairs={{0,1},{1,0},{2,3},{3,2},{4,5},{5,4},{6,7},{7,6},{8,9},{9,8},{10,11... | collective-permute-start | bytes 3145736 | tf_op jit(solution)/shard_map/ppermute | solution.py:133
  600.6 19.4 %collective-permute-start.39 = (bf16[128,1024]{0,1:T(8,128)(2,1)S(1)}, bf16[128,1024]{0,1:T(8,128)(2,1)S(1)}, u32[]{:S(2)}, u32[]{:S(2)}) collective-permute-start(bf16[128,1024]{0,1:T(8,128)(2,1)S(1)} %get-tuple-element.88), channel_id=1, source_target_pairs={{8,0},{16,8},{24,16},{28,24},{20,28},{12,20},{4,12},{0,4},{9,1},{1... | collective-permute-start | bytes 786440 | tf_op jit(solution)/shard_map/ppermute | solution.py:124
  604.8 19.2 %collective-permute-start.37 = (bf16[128,1024]{0,1:T(8,128)(2,1)S(1)}, bf16[128,1024]{0,1:T(8,128)(2,1)S(1)}, u32[]{:S(2)}, u32[]{:S(2)}) collective-permute-start(bf16[128,1024]{0,1:T(8,128)(2,1)S(1)} %get-tuple-element.87), channel_id=1, source_target_pairs={{0,8},{8,16},{16,24},{24,28},{28,20},{20,12},{12,4},{4,0},{1,9},{9... | collective-permute-start | bytes 786440 | tf_op jit(solution)/shard_map/ppermute | solution.py:124
  620.1 20.3 %collective-permute-start.40 = (bf16[128,1024]{0,1:T(8,128)(2,1)S(1)}, bf16[128,1024]{0,1:T(8,128)(2,1)S(1)}, u32[]{:S(2)}, u32[]{:S(2)}) collective-permute-start(bf16[128,1024]{0,1:T(8,128)(2,1)S(1)} %add_convert_fusion.8), channel_id=1, source_target_pairs={{8,0},{16,8},{24,16},{28,24},{20,28},{12,20},{4,12},{0,4},{9,1},{1... | collective-permute-start | bytes 786440 | tf_op jit(solution)/shard_map/ppermute | solution.py:124
  622.0 20.1 %collective-permute-start.33 = (bf16[1024,1,256]{2,0,1:T(8,128)(2,1)S(1)}, bf16[1024,1,256]{2,0,1:T(8,128)(2,1)S(1)}, u32[]{:S(2)}, u32[]{:S(2)}) collective-permute-start(bf16[1024,1,256]{2,0,1:T(8,128)(2,1)S(1)} %dynamic-slice_convert_fusion), channel_id=1, source_target_pairs={{0,2},{1,3},{2,0},{3,1},{4,6},{5,7},{6,4},{7,5},{8,10},{9,11},{10,... | collective-permute-start | bytes 1572872 | tf_op jit(solution)/shard_map/ppermute | solution.py:133
  (122 other events, 954.7 us)
Sparse Core Ops, SparseCore 0:
  35.8 79.3 all-gather.1
  466.3 123.3 all-reduce.2
  593.3 100.0 reduce-scatter.3
